TPU v7x, 32 devices: a whole 2x2x4 slice. The times are simulated.
32 devices in a mesh: expert: 16 (over z, y, core), half: 2 (over x).
Axes of the slice: x: 2, y: 2, z: 4, core: 2. Of those that a mesh axis runs over, the one named last changes fastest.
Arguments:
- tokens: bfloat16 [256, 2048], P('expert', 'half'), may hold values from -6 to 6
- upstream: bfloat16 [256, 2048], P('expert', 'half'), may hold values from -6 to 6
- expert_ids: int32 [256, 8], P('expert'), may hold values from 0 to 15, all different within a row; in each aligned block of 16 rows (0 to 15, 16 to 31, ...) at most 16 rows name the same one
- gate_probs: float32 [256, 8], P('expert'), may hold values from 0.01 to 1
- pad_mask: int32 [256], P('expert'), may hold values 0 or 1
- gate_weight: bfloat16 [16, 2048, 1536], P('expert', None, 'half'), may hold values from -0.125 to 0.125
- up_weight: bfloat16 [16, 2048, 1536], P('expert', None, 'half'), may hold values from -0.125 to 0.125
- down_weight: bfloat16 [16, 1536, 2048], P('expert', 'half'), may hold values from -0.15625 to 0.15625
Outputs:
- layer_out: bfloat16 [256, 2048], P('expert', 'half')
- grad_tokens: bfloat16 [256, 2048], P('expert', 'half')
Inputs may be any that keep to these rules, and one draw needn't show every extreme that they name: `expert_ids`: each row names 8 different experts. In the rows of one device (aligned blocks of 16 rows) no expert is named more than 16 times, a bound that some block reaches.
All inputs are finite; a program needn't handle non-finite values. No bound on the sum of `pad_mask` on one device may be relied on, other than what follows from the above.
Results may differ from a plain program's by a relative error of at most 0.025.
Values may be sent and summed in bfloat16 or wider, within the bound.
A program may use at most 64 MiB of HBM per device.

v0:
```python
import math

import jax
import jax.numpy as jnp
from jax import lax
from jax.sharding import PartitionSpec as P

orth_weight = 0.25


def assign_slots(expert_ids, experts, capacity):
    tok_count, top_count = expert_ids.shape
    flat_ids = expert_ids.reshape(tok_count * top_count)
    onehot = (flat_ids[:, None] == jnp.arange(experts, dtype=jnp.int32)[None, :]).astype(jnp.int32)
    before = jnp.cumsum(onehot, axis=0) - onehot
    slot_index = jnp.sum(before * onehot, axis=1)
    return flat_ids * capacity + slot_index


def placement_matrix(slot_dest, slots_total):
    row_index = jnp.arange(slots_total, dtype=jnp.int32)
    return (row_index[:, None] == slot_dest[None, :]).astype(jnp.bfloat16)


def to_experts(place, items):
    whole = lax.all_gather(items, "half", axis=1, tiled=True)
    buckets = jnp.dot(place, whole, preferred_element_type=jnp.float32).astype(jnp.bfloat16)
    return lax.all_to_all(buckets, "expert", split_axis=0, concat_axis=0, tiled=True)


def to_homes(partial_value):
    summed = lax.psum_scatter(
        partial_value.astype(jnp.bfloat16), "half", scatter_dimension=1, tiled=True
    )
    return lax.all_to_all(summed, "expert", split_axis=0, concat_axis=0, tiled=True)


def shards(tokens, upstream, expert_ids, gate_probs, pad_mask, gate_weight, up_weight, down_weight):
    tok_count, top_count = expert_ids.shape
    experts = lax.axis_size("expert")
    capacity = min(tok_count, 2 * tok_count * top_count // experts)
    slots_total = experts * capacity
    full_width = tokens.shape[1] * lax.axis_size("half")
    slot_dest = assign_slots(expert_ids, experts, capacity)
    place_items = placement_matrix(slot_dest, slots_total)
    place_tokens = jnp.sum(place_items.reshape(slots_total, tok_count, top_count), axis=2)
    weight_gate = gate_weight[0]
    weight_up = up_weight[0]
    weight_down = down_weight[0]
    rows_in = to_experts(place_tokens, tokens)
    gate_val = jnp.dot(rows_in, weight_gate, preferred_element_type=jnp.float32)
    up_val = jnp.dot(rows_in, weight_up, preferred_element_type=jnp.float32)
    hidden_act = (jax.nn.silu(gate_val) * up_val).astype(jnp.bfloat16)
    partial_value = jnp.dot(hidden_act, weight_down, preferred_element_type=jnp.float32)
    out_home = to_homes(partial_value)
    outputs = jnp.take(out_home, slot_dest, axis=0).reshape(tok_count, top_count, -1)
    out_float = outputs.astype(jnp.float32)
    shares = gate_probs / jnp.sum(gate_probs, axis=1, keepdims=True)
    layer_out = jnp.sum(shares[:, :, None] * out_float, axis=1).astype(jnp.bfloat16)
    gram_part = jnp.einsum("tjd,tkd->tjk", out_float, out_float) / math.sqrt(full_width)
    gram = lax.psum(gram_part, "half")
    off_diag = 1.0 - jnp.eye(top_count, dtype=jnp.float32)
    coeffs = orth_weight * gram * off_diag
    grad_out = pad_mask.astype(jnp.float32)[:, None, None] * (
        shares[:, :, None] * upstream.astype(jnp.float32)[:, None, :]
        + jnp.einsum("tjk,tkd->tjd", coeffs, out_float)
    )
    grad_items = grad_out.astype(jnp.bfloat16).reshape(tok_count * top_count, -1)
    grad_rows = to_experts(place_items, grad_items)
    grad_act = jnp.einsum("rd,hd->rh", grad_rows, weight_down, preferred_element_type=jnp.float32)
    sigma = jax.nn.sigmoid(gate_val)
    grad_gate = (grad_act * up_val * sigma * (1.0 + gate_val * (1.0 - sigma))).astype(jnp.bfloat16)
    grad_up = (grad_act * gate_val * sigma).astype(jnp.bfloat16)
    grad_partial = jnp.einsum(
        "rh,dh->rd", grad_gate, weight_gate, preferred_element_type=jnp.float32
    )
    grad_partial = grad_partial + jnp.einsum(
        "rh,dh->rd", grad_up, weight_up, preferred_element_type=jnp.float32
    )
    grad_home = to_homes(grad_partial)
    grad_pairs = jnp.take(grad_home, slot_dest, axis=0).reshape(tok_count, top_count, -1)
    grad_tokens = jnp.sum(grad_pairs.astype(jnp.float32), axis=1).astype(jnp.bfloat16)
    return (layer_out, grad_tokens)


def solution(mesh):
    in_specs = (
        P("expert", "half"),
        P("expert", "half"),
        P("expert", None),
        P("expert", None),
        P("expert"),
        P("expert", None, "half"),
        P("expert", None, "half"),
        P("expert", "half", None),
    )
    out_specs = (P("expert", "half"), P("expert", "half"))
    return jax.shard_map(shards, mesh=mesh, in_specs=in_specs, out_specs=out_specs, check_vma=False)
```

profile of v0, /device:TPU:0, one launch (start us, length us, event | category | flops | bytes accessed | tf_op | source)
XLA Modules:
  0.0 199.5 jit_solution(7568112005098671474)
XLA Ops:
  7.2 0.0 copy-start
  7.2 0.0 reduce-scatter.3.cloned.1.call-start
  7.2 0.9 copy.17
  8.1 0.1 eq.43
  8.2 0.1 fusion.33
  8.3 0.2 reduce_window_sum.11
  8.5 0.2 select_reduce_fusion
  8.7 0.1 reduce_sum.55
  8.7 0.0 copy-start.6
  8.8 0.1 fusion.30
  8.9 5.9 %all_gather.6 = bf16[16,2048]{1,0:T(8,128)(2,1)S(1)} all-gather(bf16[16,1024]{1,0:T(8,128)(2,1)} %param.10), channel_id=1, replica_groups=mesh['expert'=16,'half'=2] {'half'}, dimensions={1}, use_global_device_ids=true | all-gather | bytes 98304 | tf_op jit(solution)/shard_map/all_gather | solution.py:26
  14.8 0.4 convolution_convert_fusion.1
  15.2 30.9 %all_to_all.48 = bf16[16,16,2048]{2,1,0:T(8,128)(2,1)S(1)} all-to-all(bf16[16,16,2048]{2,1,0:T(8,128)(2,1)S(1)} %bitcast.45), channel_id=1, replica_groups=mesh['expert'=16,'half'=2] {'expert'}, dimensions={0} | all-to-all | bytes 2097152 | tf_op jit(solution)/shard_map/all_to_all | solution.py:28
  46.2 1.0 fusion.10
  47.2 0.9 copy-done.4
  48.1 1.0 fusion.6
  49.1 0.9 copy-done.11
  50.0 0.0 copy-done
  50.0 2.0 %fusion.18 = bf16[256,2048]{1,0:T(8,128)(2,1)} fusion(bf16[1,768,2048]{2,1,0:T(8,128)(2,1)S(1)} %copy-done, f32[256,768]{1,0:T(8,128)S(1)} %fusion.6, f32[256,768]{1,0:T(8,128)S(1)} %fusion.10), kind=kOutput, calls=%fused_computation.17 | convolution fusion | flops 807010304 | bytes 5767168 | tf_op jit(solution)/shard_map/dot_general | solution.py:54
  52.0 0.0 reduce-scatter.3.cloned.1.call-update
  52.0 20.9 %reduce-scatter.3.cloned.1.call-done = bf16[256,1024]{1,0:T(8,128)(2,1)} async-done(((bf16[256,2048]{1,0:T(8,128)(2,1)}), bf16[256,1024]{1,0:T(8,128)(2,1)}) %reduce-scatter.3.cloned.1.call-update) | async-done | bytes 524304 | tf_op jit(solution)/shard_map/reduce_scatter | solution.py:32
  72.9 5.7 %all-to-all-start.1 = ((bf16[16,16,1024]{2,1,0:T(8,128)(2,1)}), bf16[16,16,1024]{2,1,0:T(8,128)(2,1)}, u32[]{:S(2)}, u32[]{:S(2)}) async-start(bf16[16,16,1024]{2,1,0:T(8,128)(2,1)} %bitcast.50), calls=%async_computation.2 | async-start | bytes 1048576 | tf_op jit(solution)/shard_map/all_to_all | solution.py:35
  78.6 0.0 reduce-scatter.5.cloned.1.call-start
  78.7 0.5 convert_element_type.61
  79.2 0.1 copy.16
  79.3 0.6 subtract_multiply_fusion
  79.9 13.0 %all-to-all-done.1 = bf16[16,16,1024]{2,1,0:T(8,128)(2,1)} async-done(((bf16[16,16,1024]{2,1,0:T(8,128)(2,1)}), bf16[16,16,1024]{2,1,0:T(8,128)(2,1)}, u32[]{:S(2)}, u32[]{:S(2)}) %all-to-all-start.1) | async-done | bytes 524320 | tf_op jit(solution)/shard_map/all_to_all | solution.py:35
  92.9 2.2 %gather_fusion = bf16[128,1024]{1,0:T(8,128)(2,1)S(1)} fusion(bf16[256,1024]{1,0:T(8,128)(2,1)} %bitcast.6, s32[1024]{0:T(1024)S(1)} %pad_clamp_fusion), kind=kCustom, calls=%fused_computation.clone | custom fusion | bytes 524800 | tf_op jit(solution)/shard_map/jit(_take)/gather | solution.py:56
  95.1 1.0 convolution_multiply_fusion
  96.1 8.5 %psum.7 = f32[16,8,8]{2,1,0:T(8,128)S(1)} all-reduce(f32[16,8,8]{2,1,0:T(8,128)} %convolution_multiply_fusion), channel_id=1, replica_groups=mesh['expert'=16,'half'=2] {'half'}, use_global_device_ids=true, to_apply=%region_6.8 | all-reduce | flops 1024 | bytes 8192 | tf_op jit(solution)/shard_map/psum | solution.py:61
  104.6 1.0 fusion.23
  105.5 7.0 %all_gather.7 = bf16[128,2048]{1,0:T(8,128)(2,1)S(1)} all-gather(bf16[128,1024]{1,0:T(8,128)(2,1)S(1)} %fusion.23), channel_id=1, replica_groups=mesh['expert'=16,'half'=2] {'half'}, dimensions={1}, use_global_device_ids=true | all-gather | bytes 786432 | tf_op jit(solution)/shard_map/all_gather | solution.py:26
  112.6 1.1 convolution_convert_fusion
  113.7 28.9 %all_to_all.49 = bf16[16,16,2048]{2,1,0:T(8,128)(2,1)S(1)} all-to-all(bf16[16,16,2048]{2,1,0:T(8,128)(2,1)S(1)} %bitcast.46), channel_id=1, replica_groups=mesh['expert'=16,'half'=2] {'expert'}, dimensions={0} | all-to-all | bytes 2097152 | tf_op jit(solution)/shard_map/all_to_all | solution.py:28
  142.6 1.0 fusion
  143.6 0.9 copy-done.5
  144.4 0.2 copy-done.10
  144.6 1.0 fusion.4
  145.7 0.8 copy-done.7
  146.5 0.2 copy-done.12
  146.7 2.1 %fusion.15 = bf16[256,2048]{1,0:T(8,128)(2,1)} fusion(f32[256,2048]{1,0:T(8,128)S(1)} %fusion.4, bf16[1,2048,768]{2,1,0:T(8,128)(2,1)S(1)} %copy-done.7, f32[256,768]{1,0:T(8,128)S(1)} %copy-done.10, f32[256,768]{1,0:T(8,128)S(1)} %fusion, f32[256,768]{1,0:T(8,128)S(1)} %copy-done.12), kind=kOutput, calls=%fused_computation.15 | convolution fusion | flops 808321024 | bytes 8650752 | tf_op jit(solution)/shard_map/rh,dh->rd/dot_general | solution.py:74
  148.8 0.0 reduce-scatter.5.cloned.1.call-update
  148.8 20.9 %reduce-scatter.5.cloned.1.call-done = bf16[256,1024]{1,0:T(8,128)(2,1)} async-done(((bf16[256,2048]{1,0:T(8,128)(2,1)}), bf16[256,1024]{1,0:T(8,128)(2,1)}) %reduce-scatter.5.cloned.1.call-update) | async-done | bytes 524304 | tf_op jit(solution)/shard_map/reduce_scatter | solution.py:32
  169.7 5.7 %all-to-all-start.3 = ((bf16[16,16,1024]{2,1,0:T(8,128)(2,1)}), bf16[16,16,1024]{2,1,0:T(8,128)(2,1)}, u32[]{:S(2)}, u32[]{:S(2)}) async-start(bf16[16,16,1024]{2,1,0:T(8,128)(2,1)} %bitcast.51), calls=%async_computation.5 | async-start | bytes 1048576 | tf_op jit(solution)/shard_map/all_to_all | solution.py:35
  175.4 0.9 multiply_reduce_fusion
  176.3 13.4 %all-to-all-done.3 = bf16[16,16,1024]{2,1,0:T(8,128)(2,1)} async-done(((bf16[16,16,1024]{2,1,0:T(8,128)(2,1)}), bf16[16,16,1024]{2,1,0:T(8,128)(2,1)}, u32[]{:S(2)}, u32[]{:S(2)}) %all-to-all-start.3) | async-done | bytes 524320 | tf_op jit(solution)/shard_map/all_to_all | solution.py:35
  189.7 2.2 %gather_fusion.1 = bf16[128,1024]{1,0:T(8,128)(2,1)S(1)} fusion(bf16[256,1024]{1,0:T(8,128)(2,1)} %bitcast.12, s32[1024]{0:T(1024)S(1)} %pad_clamp_fusion), kind=kCustom, calls=%fused_computation.1.clone | custom fusion | bytes 524800 | tf_op jit(solution)/shard_map/jit(_take)/gather | solution.py:81
  191.9 0.8 bitcast_reduce_fusion
  (24 shorter events, 0.1 us)
Async XLA Ops:
  7.2 42.8 %copy-start = (bf16[1,768,2048]{2,1,0:T(8,128)(2,1)S(1)}, bf16[1,768,2048]{2,1,0:T(8,128)(2,1)}, u32[]{:S(2)}) copy-start(bf16[1,768,2048]{2,1,0:T(8,128)(2,1)} %param.17) | copy-start | bytes 9437188
  7.2 65.7 %reduce-scatter.3.cloned.1.call-start = ((), (), s32[]{:S(2)}) async-start(), calls=%async_computation.6 | async-start | bytes 1572864 | tf_op jit(solution)/shard_map/reduce_scatter | solution.py:32
  8.7 37.4 %copy-start.6 = (bf16[1,2048,768]{2,1,0:T(8,128)(2,1)S(1)}, bf16[1,2048,768]{2,1,0:T(8,128)(2,1)}, u32[]{:S(2)}) copy-start(bf16[1,2048,768]{2,1,0:T(8,128)(2,1)} %param.15) | copy-start | bytes 9437188
  46.2 1.9 copy-start.4
  48.1 1.0 copy-start.9
  49.1 0.9 copy-start.11
  50.0 28.7 %copy-start.8 = (s32[16]{0:T(128)S(1)}, s32[16]{0:T(128)}, u32[]{:S(2)}) copy-start(s32[16]{0:T(128)} %param.14) | copy-start | bytes 196
  50.0 29.2 %copy-start.2 = (f32[16,8]{0,1:T(8,128)S(1)}, f32[16,8]{0,1:T(8,128)}, u32[]{:S(2)}) copy-start(f32[16,8]{0,1:T(8,128)} %param.13) | copy-start | bytes 1540
  50.0 29.3 %copy-start.1 = (bf16[16,1024]{1,0:T(8,128)(2,1)S(1)}, bf16[16,1024]{1,0:T(8,128)(2,1)}, u32[]{:S(2)}) copy-start(bf16[16,1024]{1,0:T(8,128)(2,1)} %param.11) | copy-start | bytes 98308
  72.9 20.0 %all-to-all-start.1 = ((bf16[16,16,1024]{2,1,0:T(8,128)(2,1)}), bf16[16,16,1024]{2,1,0:T(8,128)(2,1)}, u32[]{:S(2)}, u32[]{:S(2)}) async-start(bf16[16,16,1024]{2,1,0:T(8,128)(2,1)} %bitcast.50), calls=%async_computation.2 | async-start | bytes 1048576 | tf_op jit(solution)/shard_map/all_to_all | solution.py:35
  78.6 91.1 %reduce-scatter.5.cloned.1.call-start = ((), (), s32[]{:S(2)}) async-start(), calls=%async_computation.7 | async-start | bytes 1572864 | tf_op jit(solution)/shard_map/reduce_scatter | solution.py:32
  79.9 13.0 %copy-start.3 = (s32[128]{0:T(128)}, s32[128]{0:T(128)S(1)}, u32[]{:S(2)}) copy-start(s32[128]{0:T(128)S(1)} %get-tuple-element.4) | copy-start | bytes 1540
  142.6 1.9 copy-start.5
  142.6 2.1 %copy-start.10 = (f32[256,768]{1,0:T(8,128)S(1)}, f32[256,768]{1,0:T(8,128)}, u32[]{:S(2)}) copy-start(f32[256,768]{1,0:T(8,128)} %copy-done.9) | copy-start | bytes 2359300
  144.6 1.9 copy-start.7
  144.6 2.1 %copy-start.12 = (f32[256,768]{1,0:T(8,128)S(1)}, f32[256,768]{1,0:T(8,128)}, u32[]{:S(2)}) copy-start(f32[256,768]{1,0:T(8,128)} %copy-done.11) | copy-start | bytes 2359300
  169.7 20.0 %all-to-all-start.3 = ((bf16[16,16,1024]{2,1,0:T(8,128)(2,1)}), bf16[16,16,1024]{2,1,0:T(8,128)(2,1)}, u32[]{:S(2)}, u32[]{:S(2)}) async-start(bf16[16,16,1024]{2,1,0:T(8,128)(2,1)} %bitcast.51), calls=%async_computation.5 | async-start | bytes 1048576 | tf_op jit(solution)/shard_map/all_to_all | solution.py:35
Sparse Core Ops, SparseCore 0:
  52.1 20.7 reduce-scatter.2
  148.9 20.7 reduce-scatter.4
where the time goes:
time: 200 us
  blocking collectives  81.2 us (41%)
  waiting for transfers between devices  68.2 us (34%)
  between operations  14.2 us (7%)
  matrix products  11.6 us (6%)
  starting transfers between devices  11.4 us (6%)
  local copies, waits for them, and re-layouts  9.37 us (5%)
  other arithmetic  3.43 us (2%)
    all_to_all x2, blocking collectives, to_experts(): lax.all_to_all(buckets, 'expert', split_axis=0, concat_axis=0, tiled=True)  59.8 us
    reduce_scatter x2, waiting for transfers between devices, to_homes(): lax.psum_scatter(partial_value.astype(jnp.bfloat16), 'half', scatter_dime...  41.8 us
    all_to_all x2, waiting for transfers between devices, to_homes(): lax.all_to_all(summed, 'expert', split_axis=0, concat_axis=0, tiled=True)  26.4 us
    all_gather x2, blocking collectives, to_experts(): whole = lax.all_gather(items, 'half', axis=1, tiled=True)  12.9 us
    all_to_all x2, starting transfers between devices, to_homes(): lax.all_to_all(summed, 'expert', split_axis=0, concat_axis=0, tiled=True)  11.4 us
    psum x1, blocking collectives, shards(): gram = lax.psum(gram_part, 'half')  8.48 us
    unnamed x27, local copies, waits for them, and re-layouts  4.83 us
  transfers between devices with their start and end apart: 4, of which 4 were waited for; matrix products, arithmetic and copies ran while one was open for 1% of the time, Pallas kernels for 0%

commit v1 on v0

--- a/solution.py
+++ b/solution.py
@@ -1,8 +1,11 @@
+import functools
 import math
 
 import jax
 import jax.numpy as jnp
 from jax import lax
+from jax.experimental import pallas as pl
+from jax.experimental.pallas import tpu as pltpu
 from jax.sharding import PartitionSpec as P
 
 orth_weight = 0.25
@@ -35,10 +38,331 @@
     return lax.all_to_all(summed, "expert", split_axis=0, concat_axis=0, tiled=True)
 
 
+def block_of(width):
+    return next((b for b in (256, 128) if width % b == 0), width)
+
+
+def tiles(width, body):
+    size = block_of(width)
+
+    def step(j, carry):
+        body(pl.ds(pl.multiple_of(j * size, size), size), size)
+        return carry
+
+    lax.fori_loop(0, width // size, step, 0)
+
+
+def dot(a, b):
+    return jnp.dot(a, b, preferred_element_type=jnp.float32)
+
+
+def dot_t(a, b):
+    return lax.dot_general(a, b, (((1,), (1,)), ((), ())), preferred_element_type=jnp.float32)
+
+
+def fused_kernel(
+    n, halves,
+    tokens_ref, up_ref, ids_ref, probs_ref, pad_ref, wg_hbm, wu_hbm, wd_hbm,
+    layer_ref, gtok_ref,
+    tok_buf, wg, wu, wd, gate_v, up_v, hid, gg, gu,
+    osend, xrecv, xs, gram_s, gsend, grows, psend, prec, rsend, fin,
+    w_sem, tok_ss, tok_rs, out_ss, out_rs, gram_ss, gram_rs, grad_ss, grad_rs,
+    pair_ss, pair_rs, fin_ss, fin_rs,
+):
+    e = lax.axis_index("expert")
+    h = lax.axis_index("half")
+    tok, width = tokens_ref.shape
+    hidden = wg.shape[1]
+    rows = n * tok
+    chips = n // 2
+    parity = lax.rem(e, 2)
+    chip = lax.div(e, 2)
+    sibling = e + 1 - 2 * parity
+    full = halves * width
+
+    def remote(src, dst, ssem, rsem, pe, ph):
+        return pltpu.make_async_remote_copy(
+            src_ref=src, dst_ref=dst, send_sem=ssem, recv_sem=rsem,
+            device_id=(pe, ph), device_id_type=pl.DeviceIdType.MESH,
+        )
+
+    def wrap(a, d, size):
+        return lax.rem(a + d, size)
+
+    loads = [
+        pltpu.make_async_copy(src.at[0], dst, w_sem.at[i])
+        for i, (src, dst) in enumerate(((wg_hbm, wg), (wu_hbm, wu), (wd_hbm, wd)))
+    ]
+    for c in loads:
+        c.start()
+
+    everyone = [(de, dh) for de in range(n) for dh in range(halves) if de or dh]
+    barrier = pltpu.get_barrier_semaphore()
+    for de, dh in everyone:
+        pl.semaphore_signal(
+            barrier, inc=1, device_id=(wrap(e, de, n), wrap(h, dh, halves)),
+            device_id_type=pl.DeviceIdType.MESH,
+        )
+    pl.semaphore_wait(barrier, len(everyone))
+
+    sends = []
+    far = [(dm, dh) for dm in range(chips) for dh in range(halves) if dm or dh]
+    k = 0
+    for dm, dh in far:
+        c = remote(
+            tokens_ref, tok_buf.at[h, e], tok_ss.at[k], tok_rs.at[h, e],
+            2 * wrap(chip, dm, chips) + parity, wrap(h, dh, halves),
+        )
+        c.start()
+        sends.append(c)
+        k += 1
+    c = remote(tokens_ref, tok_buf.at[h, e], tok_ss.at[k], tok_rs.at[h, e], sibling, h)
+    c.start()
+    sends.append(c)
+    k += 1
+    tok_buf[h, e] = tokens_ref[...]
+    for dm, dh in far:
+        pe = 2 * wrap(chip, chips - dm, chips) + parity
+        ph = wrap(h, halves - dh, halves)
+        slot = tok_buf.at[ph, pe]
+        c = remote(slot, slot, tok_ss.at[k], tok_rs.at[ph, pe], sibling, h)
+        c.wait_recv()
+        c.start()
+        sends.append(c)
+        k += 1
+    slot = tok_buf.at[h, sibling]
+    remote(slot, slot, tok_ss.at[0], tok_rs.at[h, sibling], sibling, h).wait_recv()
+    for dm, dh in far:
+        pe = 2 * wrap(chip, chips - dm, chips) + 1 - parity
+        ph = wrap(h, halves - dh, halves)
+        slot = tok_buf.at[ph, pe]
+        remote(slot, slot, tok_ss.at[0], tok_rs.at[ph, pe], sibling, h).wait_recv()
+
+    loads[0].wait()
+    loads[1].wait()
+
+    def hidden_step(cols, size):
+        gate = jnp.zeros((rows, size), jnp.float32)
+        up = jnp.zeros((rows, size), jnp.float32)
+        for i in range(halves):
+            x = tok_buf[i].reshape(rows, width)
+            gate = gate + dot(x, wg[i * width:(i + 1) * width, cols])
+            up = up + dot(x, wu[i * width:(i + 1) * width, cols])
+        gate_v[:, cols] = gate
+        up_v[:, cols] = up
+        hid[:, cols] = (gate / (1.0 + jnp.exp(-gate)) * up).astype(jnp.bfloat16)
+
+    tiles(hidden, hidden_step)
+    loads[2].wait()
+
+    for i in range(halves):
+        def down_step(cols, size, i=i):
+            at = pl.ds(pl.multiple_of(cols.start + i * width, size), size)
+            part = dot(hid[...], wd[:, at])
+            osend[i, :, :, cols] = part.reshape(n, tok, size).astype(jnp.bfloat16)
+
+        tiles(width, down_step)
+
+    for k, (de, dh) in enumerate(everyone):
+        pe, ph = wrap(e, de, n), wrap(h, dh, halves)
+        c = remote(osend.at[ph, pe], xrecv.at[h, e], out_ss.at[k], out_rs.at[h, e], pe, ph)
+        c.start()
+        sends.append(c)
+    xrecv[h, e] = osend[h, e]
+
+    probs = probs_ref[...]
+    shares = probs / jnp.sum(probs, axis=1, keepdims=True)
+    ids = ids_ref[...]
+    for de, dh in everyone:
+        pe, ph = wrap(e, n - de, n), wrap(h, halves - dh, halves)
+        slot = xrecv.at[ph, pe]
+        remote(slot, slot, out_ss.at[0], out_rs.at[ph, pe], sibling, h).wait_recv()
+
+    layer = jnp.zeros((tok, width), jnp.float32)
+    share_rows = []
+    for i in range(n):
+        total = xrecv[0, i].astype(jnp.float32)
+        for j in range(1, halves):
+            total = total + xrecv[j, i].astype(jnp.float32)
+        named = jnp.sum((ids == i).astype(jnp.float32), axis=1, keepdims=True)
+        share = jnp.sum(jnp.where(ids == i, shares, 0.0), axis=1, keepdims=True)
+        value = jnp.where(named > 0.0, total, 0.0).astype(jnp.bfloat16)
+        xs[i] = value
+        layer = layer + share * value.astype(jnp.float32)
+        share_rows.append(share)
+    layer_ref[...] = layer.astype(jnp.bfloat16)
+
+    x_all = xs[...].reshape(rows, width)
+    same = (
+        lax.rem(lax.broadcasted_iota(jnp.int32, (tok, rows), 1), tok)
+        == lax.broadcasted_iota(jnp.int32, (tok, rows), 0)
+    ).astype(jnp.float32)
+    gram = dot_t(x_all, x_all).reshape(n, tok, rows) * same[None]
+    gram_s[h] = jnp.sum(gram, axis=1)
+    for dh in range(1, halves):
+        c = remote(
+            gram_s.at[h], gram_s.at[h], gram_ss.at[dh], gram_rs.at[h], e, wrap(h, dh, halves)
+        )
+        c.start()
+        sends.append(c)
+    for dh in range(1, halves):
+        ph = wrap(h, halves - dh, halves)
+        slot = gram_s.at[ph]
+        remote(slot, slot, gram_ss.at[0], gram_rs.at[ph], e, ph).wait_recv()
+    whole = gram_s[0]
+    for i in range(1, halves):
+        whole = whole + gram_s[i]
+    apart = (
+        lax.div(lax.broadcasted_iota(jnp.int32, (n, rows), 1), tok)
+        != lax.broadcasted_iota(jnp.int32, (n, rows), 0)
+    ).astype(jnp.float32)
+    whole = whole * (apart * (orth_weight / math.sqrt(full)))
+    coeffs = (whole[:, None, :] * same[None]).reshape(rows, rows)
+    high = coeffs.astype(jnp.bfloat16)
+    low = (coeffs - high.astype(jnp.float32)).astype(jnp.bfloat16)
+    pad = pad_ref[...].astype(jnp.float32)
+
+    def grad_step(cols, size):
+        x = xs[:, :, cols].reshape(rows, size)
+        mixed = (dot(high, x) + dot(low, x)).reshape(n, tok, size)
+        upstream = up_ref[:, cols].astype(jnp.float32)
+        for i in range(n):
+            gsend[i, :, cols] = (pad * (share_rows[i] * upstream + mixed[i])).astype(jnp.bfloat16)
+
+    tiles(width, grad_step)
+
+    for k, (de, dh) in enumerate(everyone):
+        pe, ph = wrap(e, de, n), wrap(h, dh, halves)
+        c = remote(gsend.at[pe], grows.at[h, e], grad_ss.at[k], grad_rs.at[h, e], pe, ph)
+        c.start()
+        sends.append(c)
+    grows[h, e] = gsend[e]
+    for de, dh in everyone:
+        pe, ph = wrap(e, n - de, n), wrap(h, halves - dh, halves)
+        slot = grows.at[ph, pe]
+        remote(slot, slot, grad_ss.at[0], grad_rs.at[ph, pe], sibling, h).wait_recv()
+
+    def act_step(cols, size):
+        act = jnp.zeros((rows, size), jnp.float32)
+        for i in range(halves):
+            g = grows[i].reshape(rows, width)
+            act = act + dot_t(g, wd[cols, i * width:(i + 1) * width])
+        gate = gate_v[:, cols]
+        sigma = 1.0 / (1.0 + jnp.exp(-gate))
+        gg[:, cols] = (
+            act * up_v[:, cols] * sigma * (1.0 + gate * (1.0 - sigma))
+        ).astype(jnp.bfloat16)
+        gu[:, cols] = (act * gate * sigma).astype(jnp.bfloat16)
+
+    tiles(hidden, act_step)
+
+    for i in range(halves):
+        def back_step(cols, size, i=i):
+            at = pl.ds(pl.multiple_of(cols.start + i * width, size), size)
+            part = dot_t(gg[...], wg[at, :]) + dot_t(gu[...], wu[at, :])
+            part = part.astype(jnp.bfloat16).reshape(chips, 2, tok, size)
+            for q in range(2):
+                psend[q, i, :, :, cols] = part[:, q]
+
+        tiles(width, back_step)
+
+    c = remote(psend.at[1 - parity], prec, pair_ss, pair_rs, sibling, h)
+    c.start()
+    sends.append(c)
+    c.wait_recv()
+    for i in range(halves):
+        for m in range(chips):
+            rsend[i, m] = (
+                psend[parity, i, m].astype(jnp.float32) + prec[i, m].astype(jnp.float32)
+            ).astype(jnp.bfloat16)
+    for k, (dm, dh) in enumerate(far):
+        pm, ph = wrap(chip, dm, chips), wrap(h, dh, halves)
+        c = remote(
+            rsend.at[ph, pm], fin.at[h, chip], fin_ss.at[k], fin_rs.at[h, chip],
+            2 * pm + parity, ph,
+        )
+        c.start()
+        sends.append(c)
+    fin[h, chip] = rsend[h, chip]
+    for dm, dh in far:
+        pm, ph = wrap(chip, chips - dm, chips), wrap(h, halves - dh, halves)
+        slot = fin.at[ph, pm]
+        remote(slot, slot, fin_ss.at[0], fin_rs.at[ph, pm], sibling, h).wait_recv()
+    total = jnp.zeros((tok, width), jnp.float32)
+    for i in range(halves):
+        for m in range(chips):
+            total = total + fin[i, m].astype(jnp.float32)
+    gtok_ref[...] = total.astype(jnp.bfloat16)
+    for c in sends:
+        c.wait_send()
+
+
+def fused(tokens, upstream, expert_ids, gate_probs, pad_mask, gate_weight, up_weight, down_weight):
+    n, halves = lax.axis_size("expert"), lax.axis_size("half")
+    tok, width = tokens.shape
+    hidden = gate_weight.shape[2]
+    rows, full, chips = n * tok, halves * width, n // 2
+    low, wide = jnp.bfloat16, jnp.float32
+    vmem, dma = pltpu.VMEM, pltpu.SemaphoreType.DMA
+    local = pl.BlockSpec(memory_space=pltpu.VMEM)
+    remain = pl.BlockSpec(memory_space=pl.ANY)
+    return pl.pallas_call(
+        functools.partial(fused_kernel, n, halves),
+        out_shape=[jax.ShapeDtypeStruct((tok, width), low)] * 2,
+        in_specs=[local] * 5 + [remain] * 3,
+        out_specs=[local] * 2,
+        scratch_shapes=[
+            vmem((halves, n, tok, width), low),
+            vmem((full, hidden), low),
+            vmem((full, hidden), low),
+            vmem((hidden, full), low),
+            vmem((rows, hidden), wide),
+            vmem((rows, hidden), wide),
+            vmem((rows, hidden), low),
+            vmem((rows, hidden), low),
+            vmem((rows, hidden), low),
+            vmem((halves, n, tok, width), low),
+            vmem((halves, n, tok, width), low),
+            vmem((n, tok, width), low),
+            vmem((halves, n, rows), wide),
+            vmem((n, tok, width), low),
+            vmem((halves, n, tok, width), low),
+            vmem((2, halves, chips, tok, width), low),
+            vmem((halves, chips, tok, width), low),
+            vmem((halves, chips, tok, width), low),
+            vmem((halves, chips, tok, width), low),
+            dma((3,)),
+            dma((halves * n,)),
+            dma((halves, n)),
+            dma((halves * n,)),
+            dma((halves, n)),
+            dma((halves,)),
+            dma((halves,)),
+            dma((halves * n,)),
+            dma((halves, n)),
+            dma,
+            dma,
+            dma((halves * chips,)),
+            dma((halves, chips)),
+        ],
+        compiler_params=pltpu.CompilerParams(
+            collective_id=0, has_side_effects=True, vmem_limit_bytes=56 * 1024 * 1024
+        ),
+        name="experts",
+    )(
+        tokens, upstream, expert_ids, gate_probs, pad_mask.reshape(tok, 1),
+        gate_weight, up_weight, down_weight,
+    )
+
+
 def shards(tokens, upstream, expert_ids, gate_probs, pad_mask, gate_weight, up_weight, down_weight):
     tok_count, top_count = expert_ids.shape
     experts = lax.axis_size("expert")
     capacity = min(tok_count, 2 * tok_count * top_count // experts)
+    if capacity == tok_count and experts % 2 == 0:
+        return fused(
+            tokens, upstream, expert_ids, gate_probs, pad_mask, gate_weight, up_weight, down_weight
+        )
     slots_total = experts * capacity
     full_width = tokens.shape[1] * lax.axis_size("half")
     slot_dest = assign_slots(expert_ids, experts, capacity)

time: 200 us -> 102 us (0.51)
  Pallas kernels: 0 us -> 92.9 us
  blocking collectives: 81.2 us -> 0 us
  waiting for transfers between devices: 68.2 us -> 0 us
  between operations: 14.2 us -> 0.64 us
  matrix products: 11.6 us -> 0 us
  starting transfers between devices: 11.4 us -> 0 us
  other arithmetic: 3.43 us -> 0 us
  local copies, waits for them, and re-layouts: 9.37 us -> 6.79 us
    pallas_call x0 -> x1, Pallas kernels: none -> 92.9 us  [fused(): pl.pallas_call(functools.partial(fused_kernel, n, halves), out_shape=[jax...]
    all_to_all x2 -> x0, blocking collectives: 59.8 us -> none  [to_experts(): lax.all_to_all(buckets, 'expert', split_axis=0, concat_axis=0, tiled=True)]
    reduce_scatter x2 -> x0, waiting for transfers between devices: 41.8 us -> none  [to_homes(): lax.psum_scatter(partial_value.astype(jnp.bfloat16), 'half', scatter_dime...]
    all_to_all x2 -> x0, waiting for transfers between devices: 26.4 us -> none  [to_homes(): lax.all_to_all(summed, 'expert', split_axis=0, concat_axis=0, tiled=True)]
    all_gather x2 -> x0, blocking collectives: 12.9 us -> none  [to_experts(): whole = lax.all_gather(items, 'half', axis=1, tiled=True)]
    dot_general x10 -> x0, matrix products: 11.6 us -> none  [the longest x1 2.08 us: shards(): jnp.einsum('rh,dh->rd', grad_gate, weight_gate, preferred_element_type=jn...]
    all_to_all x2 -> x0, starting transfers between devices: 11.4 us -> none  [to_homes(): lax.all_to_all(summed, 'expert', split_axis=0, concat_axis=0, tiled=True)]
    psum x1 -> x0, blocking collectives: 8.48 us -> none  [shards(): gram = lax.psum(gram_part, 'half')]
  transfers between devices with their start and end apart: 4 -> 0, of which waited for: 4 -> 0; matrix products, arithmetic and copies ran while one was open for 1% -> 0% of each run, Pallas kernels for 0% -> 0%
where the time goes in v1:
time: 102 us; the launch traced here: 100 us
  Pallas kernels  92.9 us (91%)
  local copies, waits for them, and re-layouts  6.79 us (7%)
    pallas_call x1, Pallas kernels, fused(): pl.pallas_call(functools.partial(fused_kernel, n, halves), out_shape=[jax...  92.9 us
    unnamed x4, local copies, waits for them, and re-layouts  5.46 us

profile of v1, /device:TPU:0, one launch (start us, length us, event | category | flops | bytes accessed | tf_op | source)
XLA Modules:
  0.0 100.4 jit_solution(8851200223223044897)
XLA Ops:
  0.6 1.4 %copy.10.ids_ref = s32[16,8]{1,0:T(8,128)} copy(s32[16,8]{0,1:T(8,128)} %param.10) | data formatting | bytes 1024 | tf_op args[2]
  2.0 1.4 %copy.11.probs_ref = f32[16,8]{1,0:T(8,128)} copy(f32[16,8]{0,1:T(8,128)} %param.11) | data formatting | bytes 1024 | tf_op args[3]
  3.3 1.3 %copy.12.pad_ref = s32[16,1]{1,0:T(8,128)} copy(s32[16,1]{0,1:T(1,128)} %bitcast.1) | data formatting | bytes 128 | tf_op jit(solution)/shard_map/reshape | solution.py:353
  4.7 92.9 %experts.1 = (bf16[16,1024]{1,0:T(8,128)(2,1)}, bf16[16,1024]{1,0:T(8,128)(2,1)}) custom-call(bf16[16,1024]{1,0:T(8,128)(2,1)} %tokens_ref.1, bf16[16,1024]{1,0:T(8,128)(2,1)} %up_ref.1, s32[16,8]{1,0:T(8,128)} %copy.10.ids_ref, f32[16,8]{1,0:T(8,128)} %copy.11.probs_ref, s32[16,1]{1,0:T(8,128)} %copy.12.pad_ref, bf16[1,2048,768]{2,1,0:T(8,128)(2,1)} %wg_hbm.1, ...), custom_call_target="tpu_custom_call" | custom-call | tf_op jit(solution)/shard_map/experts/pallas_call | solution.py:309
  97.6 1.4 %copy.15 = bf16[16,1024]{1,0:T(8,128)(2,1)} copy(bf16[16,1024]{1,0:T(8,128)(2,1)} %get-tuple-element.4) | data formatting | bytes 65536
  99.0 1.4 %copy.16 = bf16[16,1024]{1,0:T(8,128)(2,1)} copy(bf16[16,1024]{1,0:T(8,128)(2,1)} %get-tuple-element.5) | data formatting | bytes 65536

commit v2 on v1

--- a/solution.py
+++ b/solution.py
@@ -60,18 +60,24 @@
     return lax.dot_general(a, b, (((1,), (1,)), ((), ())), preferred_element_type=jnp.float32)
 
 
+def copy_kernel(a_ref, b_ref, a_out, b_out):
+    a_out[...] = a_ref[...]
+    b_out[...] = b_ref[...]
+
+
 def fused_kernel(
     n, halves,
-    tokens_ref, up_ref, ids_ref, probs_ref, pad_ref, wg_hbm, wu_hbm, wd_hbm,
+    tok_hbm, up_hbm, ids_hbm, probs_hbm, pad_hbm, wg_hbm, wu_hbm, wd_hbm,
     layer_ref, gtok_ref,
+    up_ref, ids_ref, probs_ref, pad_ref,
     tok_buf, wg, wu, wd, gate_v, up_v, hid, gg, gu,
-    osend, xrecv, xs, gram_s, gsend, grows, psend, prec, rsend, fin,
-    w_sem, tok_ss, tok_rs, out_ss, out_rs, gram_ss, gram_rs, grad_ss, grad_rs,
-    pair_ss, pair_rs, fin_ss, fin_rs,
+    osend, orecv, ored, xrecv, xs, gram_s, gsend, grows, psend, prec, fsend, frecv, rsend, fin,
+    w_sem, tok_ss, tok_rs, part_ss, part_rs, out_ss, out_rs, gram_ss, gram_rs,
+    grad_ss, grad_rs, relay_ss, pair_ss, pair_rs, fpart_ss, fpart_rs, fin_ss, fin_rs,
 ):
     e = lax.axis_index("expert")
     h = lax.axis_index("half")
-    tok, width = tokens_ref.shape
+    tok, width = up_ref.shape
     hidden = wg.shape[1]
     rows = n * tok
     chips = n // 2
@@ -89,57 +95,76 @@
     def wrap(a, d, size):
         return lax.rem(a + d, size)
 
-    loads = [
-        pltpu.make_async_copy(src.at[0], dst, w_sem.at[i])
-        for i, (src, dst) in enumerate(((wg_hbm, wg), (wu_hbm, wu), (wd_hbm, wd)))
-    ]
+    def arrived(slot, rsem):
+        remote(slot, slot, pair_ss.at[0], rsem, sibling, h).wait_recv()
+
+    sends = []
+
+    def send(*args):
+        c = remote(*args)
+        c.start()
+        sends.append(c)
+
+    moves = (
+        (tok_hbm, tok_buf.at[h, e]), (ids_hbm, ids_ref), (probs_hbm, probs_ref),
+        (pad_hbm, pad_ref), (up_hbm, up_ref),
+        (wg_hbm.at[0], wg), (wu_hbm.at[0], wu), (wd_hbm.at[0], wd),
+    )
+    loads = [pltpu.make_async_copy(src, dst, w_sem.at[i]) for i, (src, dst) in enumerate(moves)]
     for c in loads:
         c.start()
 
-    everyone = [(de, dh) for de in range(n) for dh in range(halves) if de or dh]
+    others = list(range(1, halves))
+    near = sorted(range(1, n), key=lambda d: (min(d, n - d), d))
+    outer = near[::-1]
+    chips_near = sorted(range(1, chips), key=lambda d: (min(d, chips - d), d))
+    chips_far = chips_near[::-1]
+
     barrier = pltpu.get_barrier_semaphore()
-    for de, dh in everyone:
+    for d in outer:
         pl.semaphore_signal(
-            barrier, inc=1, device_id=(wrap(e, de, n), wrap(h, dh, halves)),
-            device_id_type=pl.DeviceIdType.MESH,
+            barrier, inc=1, device_id=(wrap(e, d, n), h), device_id_type=pl.DeviceIdType.MESH
         )
-    pl.semaphore_wait(barrier, len(everyone))
-
-    sends = []
-    far = [(dm, dh) for dm in range(chips) for dh in range(halves) if dm or dh]
+    for d in others:
+        pl.semaphore_signal(
+            barrier, inc=1, device_id=(e, wrap(h, d, halves)), device_id_type=pl.DeviceIdType.MESH
+        )
+    pl.semaphore_wait(barrier, len(outer) + len(others))
+
+    loads[0].wait()
     k = 0
-    for dm, dh in far:
-        c = remote(
-            tokens_ref, tok_buf.at[h, e], tok_ss.at[k], tok_rs.at[h, e],
-            2 * wrap(chip, dm, chips) + parity, wrap(h, dh, halves),
-        )
-        c.start()
-        sends.append(c)
+    mine = tok_buf.at[h, e]
+    for d in chips_far:
+        send(mine, mine, tok_ss.at[k], tok_rs.at[h, e], 2 * wrap(chip, d, chips) + parity, h)
         k += 1
-    c = remote(tokens_ref, tok_buf.at[h, e], tok_ss.at[k], tok_rs.at[h, e], sibling, h)
-    c.start()
-    sends.append(c)
+    for d in others:
+        send(mine, mine, tok_ss.at[k], tok_rs.at[h, e], e, wrap(h, d, halves))
+        k += 1
+    send(mine, mine, tok_ss.at[k], tok_rs.at[h, e], sibling, h)
     k += 1
-    tok_buf[h, e] = tokens_ref[...]
-    for dm, dh in far:
-        pe = 2 * wrap(chip, chips - dm, chips) + parity
-        ph = wrap(h, halves - dh, halves)
-        slot = tok_buf.at[ph, pe]
-        c = remote(slot, slot, tok_ss.at[k], tok_rs.at[ph, pe], sibling, h)
-        c.wait_recv()
-        c.start()
-        sends.append(c)
+    for d in chips_near:
+        pe = 2 * wrap(chip, chips - d, chips) + parity
+        slot = tok_buf.at[h, pe]
+        arrived(slot, tok_rs.at[h, pe])
+        for dh in others:
+            send(slot, slot, tok_ss.at[k], tok_rs.at[h, pe], e, wrap(h, dh, halves))
+            k += 1
+        send(slot, slot, tok_ss.at[k], tok_rs.at[h, pe], sibling, h)
         k += 1
-    slot = tok_buf.at[h, sibling]
-    remote(slot, slot, tok_ss.at[0], tok_rs.at[h, sibling], sibling, h).wait_recv()
-    for dm, dh in far:
-        pe = 2 * wrap(chip, chips - dm, chips) + 1 - parity
-        ph = wrap(h, halves - dh, halves)
-        slot = tok_buf.at[ph, pe]
-        remote(slot, slot, tok_ss.at[0], tok_rs.at[ph, pe], sibling, h).wait_recv()
-
-    loads[0].wait()
-    loads[1].wait()
+    for d in [0] + chips_near:
+        pe = 2 * wrap(chip, chips - d, chips) + parity
+        for dh in others:
+            ph = wrap(h, halves - dh, halves)
+            slot = tok_buf.at[ph, pe]
+            arrived(slot, tok_rs.at[ph, pe])
+            send(slot, slot, tok_ss.at[k], tok_rs.at[ph, pe], sibling, h)
+            k += 1
+    for c in loads[1:7]:
+        c.wait()
+    for d in [0] + chips_near:
+        pe = 2 * wrap(chip, chips - d, chips) + 1 - parity
+        for ph in range(halves):
+            arrived(tok_buf.at[ph, pe], tok_rs.at[ph, pe])
 
     def hidden_step(cols, size):
         gate = jnp.zeros((rows, size), jnp.float32)
@@ -153,43 +178,68 @@
         hid[:, cols] = (gate / (1.0 + jnp.exp(-gate)) * up).astype(jnp.bfloat16)
 
     tiles(hidden, hidden_step)
-    loads[2].wait()
-
-    for i in range(halves):
-        def down_step(cols, size, i=i):
-            at = pl.ds(pl.multiple_of(cols.start + i * width, size), size)
+    loads[7].wait()
+
+    for dh in others + [0]:
+        ph = wrap(h, dh, halves)
+
+        def down_step(cols, size, ph=ph, dh=dh):
+            at = pl.ds(pl.multiple_of(cols.start + ph * width, size), size)
             part = dot(hid[...], wd[:, at])
-            osend[i, :, :, cols] = part.reshape(n, tok, size).astype(jnp.bfloat16)
+            osend[dh, :, :, cols] = part.reshape(n, tok, size).astype(jnp.bfloat16)
 
         tiles(width, down_step)
-
-    for k, (de, dh) in enumerate(everyone):
-        pe, ph = wrap(e, de, n), wrap(h, dh, halves)
-        c = remote(osend.at[ph, pe], xrecv.at[h, e], out_ss.at[k], out_rs.at[h, e], pe, ph)
-        c.start()
-        sends.append(c)
-    xrecv[h, e] = osend[h, e]
-
-    probs = probs_ref[...]
+        if dh:
+            for j, d in enumerate(outer + [0]):
+                pe = wrap(e, d, n)
+                send(
+                    osend.at[dh, pe], orecv.at[halves - dh, pe],
+                    part_ss.at[dh, j], part_rs.at[halves - dh, j], e, ph,
+                )
+
+    eye = (
+        lax.broadcasted_iota(jnp.int32, (tok, tok), 0)
+        == lax.broadcasted_iota(jnp.int32, (tok, tok), 1)
+    )
+    top = ids_ref.shape[0]
+    lane = lax.broadcasted_iota(jnp.int32, (tok, top), 1)
+
+    def column(row):
+        return jnp.sum(jnp.where(eye, jnp.broadcast_to(row, (tok, tok)), 0.0), axis=1, keepdims=True)
+
+    ids = jnp.zeros((tok, top), jnp.float32)
+    probs = jnp.zeros((tok, top), jnp.float32)
+    for j in range(top):
+        ids = jnp.where(lane == j, column(ids_ref[j:j + 1, :].astype(jnp.float32)), ids)
+        probs = jnp.where(lane == j, column(probs_ref[j:j + 1, :]), probs)
+    pad = column(pad_ref[...].astype(jnp.float32))
     shares = probs / jnp.sum(probs, axis=1, keepdims=True)
-    ids = ids_ref[...]
-    for de, dh in everyone:
-        pe, ph = wrap(e, n - de, n), wrap(h, halves - dh, halves)
-        slot = xrecv.at[ph, pe]
-        remote(slot, slot, out_ss.at[0], out_rs.at[ph, pe], sibling, h).wait_recv()
+    named_rows, share_rows = [], []
+    for i in range(n):
+        named_rows.append(jnp.sum((ids == float(i)).astype(jnp.float32), axis=1, keepdims=True))
+        share_rows.append(jnp.sum(jnp.where(ids == float(i), shares, 0.0), axis=1, keepdims=True))
+
+    for j, d in enumerate(outer + [0]):
+        pe = wrap(e, d, n)
+        total = osend[0, pe].astype(jnp.float32)
+        for dh in others:
+            arrived(orecv.at[dh, pe], part_rs.at[dh, j])
+            total = total + orecv[dh, pe].astype(jnp.float32)
+        if d:
+            ored[pe] = total.astype(jnp.bfloat16)
+            send(ored.at[pe], xrecv.at[e], out_ss.at[j], out_rs.at[e], pe, h)
+        else:
+            xrecv[e] = total.astype(jnp.bfloat16)
+    for d in near:
+        pe = wrap(e, n - d, n)
+        arrived(xrecv.at[pe], out_rs.at[pe])
 
     layer = jnp.zeros((tok, width), jnp.float32)
-    share_rows = []
     for i in range(n):
-        total = xrecv[0, i].astype(jnp.float32)
-        for j in range(1, halves):
-            total = total + xrecv[j, i].astype(jnp.float32)
-        named = jnp.sum((ids == i).astype(jnp.float32), axis=1, keepdims=True)
-        share = jnp.sum(jnp.where(ids == i, shares, 0.0), axis=1, keepdims=True)
-        value = jnp.where(named > 0.0, total, 0.0).astype(jnp.bfloat16)
-        xs[i] = value
-        layer = layer + share * value.astype(jnp.float32)
-        share_rows.append(share)
+        value = xrecv[i]
+        value = jnp.where(named_rows[i] > 0.0, value.astype(jnp.float32), 0.0)
+        xs[i] = value.astype(jnp.bfloat16)
+        layer = layer + share_rows[i] * value
     layer_ref[...] = layer.astype(jnp.bfloat16)
 
     x_all = xs[...].reshape(rows, width)
@@ -200,15 +250,10 @@
     gram = dot_t(x_all, x_all).reshape(n, tok, rows) * same[None]
     gram_s[h] = jnp.sum(gram, axis=1)
     for dh in range(1, halves):
-        c = remote(
-            gram_s.at[h], gram_s.at[h], gram_ss.at[dh], gram_rs.at[h], e, wrap(h, dh, halves)
-        )
-        c.start()
-        sends.append(c)
+        send(gram_s.at[h], gram_s.at[h], gram_ss.at[dh], gram_rs.at[h], e, wrap(h, dh, halves))
     for dh in range(1, halves):
         ph = wrap(h, halves - dh, halves)
-        slot = gram_s.at[ph]
-        remote(slot, slot, gram_ss.at[0], gram_rs.at[ph], e, ph).wait_recv()
+        arrived(gram_s.at[ph], gram_rs.at[ph])
     whole = gram_s[0]
     for i in range(1, halves):
         whole = whole + gram_s[i]
@@ -220,7 +265,6 @@
     coeffs = (whole[:, None, :] * same[None]).reshape(rows, rows)
     high = coeffs.astype(jnp.bfloat16)
     low = (coeffs - high.astype(jnp.float32)).astype(jnp.bfloat16)
-    pad = pad_ref[...].astype(jnp.float32)
 
     def grad_step(cols, size):
         x = xs[:, :, cols].reshape(rows, size)
@@ -231,16 +275,26 @@
 
     tiles(width, grad_step)
 
-    for k, (de, dh) in enumerate(everyone):
-        pe, ph = wrap(e, de, n), wrap(h, dh, halves)
-        c = remote(gsend.at[pe], grows.at[h, e], grad_ss.at[k], grad_rs.at[h, e], pe, ph)
-        c.start()
-        sends.append(c)
+    for j, d in enumerate(outer):
+        pe = wrap(e, d, n)
+        send(gsend.at[pe], grows.at[h, e], grad_ss.at[j], grad_rs.at[h, e], pe, h)
+    k = 0
+    for dh in others:
+        send(gsend.at[e], grows.at[h, e], relay_ss.at[k], grad_rs.at[h, e], e, wrap(h, dh, halves))
+        k += 1
     grows[h, e] = gsend[e]
-    for de, dh in everyone:
-        pe, ph = wrap(e, n - de, n), wrap(h, halves - dh, halves)
-        slot = grows.at[ph, pe]
-        remote(slot, slot, grad_ss.at[0], grad_rs.at[ph, pe], sibling, h).wait_recv()
+    for d in near:
+        pe = wrap(e, n - d, n)
+        slot = grows.at[h, pe]
+        arrived(slot, grad_rs.at[h, pe])
+        for dh in others:
+            send(slot, slot, relay_ss.at[k], grad_rs.at[h, pe], e, wrap(h, dh, halves))
+            k += 1
+    for d in [0] + near:
+        pe = wrap(e, n - d, n)
+        for dh in others:
+            ph = wrap(h, halves - dh, halves)
+            arrived(grows.at[ph, pe], grad_rs.at[ph, pe])
 
     def act_step(cols, size):
         act = jnp.zeros((rows, size), jnp.float32)
@@ -256,42 +310,44 @@
 
     tiles(hidden, act_step)
 
-    for i in range(halves):
-        def back_step(cols, size, i=i):
-            at = pl.ds(pl.multiple_of(cols.start + i * width, size), size)
+    for dh in others + [0]:
+        ph = wrap(h, dh, halves)
+
+        def back_step(cols, size, ph=ph, dh=dh):
+            at = pl.ds(pl.multiple_of(cols.start + ph * width, size), size)
             part = dot_t(gg[...], wg[at, :]) + dot_t(gu[...], wu[at, :])
             part = part.astype(jnp.bfloat16).reshape(chips, 2, tok, size)
             for q in range(2):
-                psend[q, i, :, :, cols] = part[:, q]
+                psend[dh, q, :, :, cols] = part[:, q]
 
         tiles(width, back_step)
-
-    c = remote(psend.at[1 - parity], prec, pair_ss, pair_rs, sibling, h)
-    c.start()
-    sends.append(c)
-    c.wait_recv()
-    for i in range(halves):
-        for m in range(chips):
-            rsend[i, m] = (
-                psend[parity, i, m].astype(jnp.float32) + prec[i, m].astype(jnp.float32)
+        send(psend.at[dh, 1 - parity], prec.at[dh], pair_ss.at[dh], pair_rs.at[dh], sibling, h)
+    order = chips_far + [0]
+    for dh in others:
+        arrived(prec.at[dh], pair_rs.at[dh])
+        for j, d in enumerate(order):
+            pm = wrap(chip, d, chips)
+            fsend[dh, pm] = (
+                psend[dh, parity, pm].astype(jnp.float32) + prec[dh, pm].astype(jnp.float32)
             ).astype(jnp.bfloat16)
-    for k, (dm, dh) in enumerate(far):
-        pm, ph = wrap(chip, dm, chips), wrap(h, dh, halves)
-        c = remote(
-            rsend.at[ph, pm], fin.at[h, chip], fin_ss.at[k], fin_rs.at[h, chip],
-            2 * pm + parity, ph,
-        )
-        c.start()
-        sends.append(c)
-    fin[h, chip] = rsend[h, chip]
-    for dm, dh in far:
-        pm, ph = wrap(chip, chips - dm, chips), wrap(h, halves - dh, halves)
-        slot = fin.at[ph, pm]
-        remote(slot, slot, fin_ss.at[0], fin_rs.at[ph, pm], sibling, h).wait_recv()
-    total = jnp.zeros((tok, width), jnp.float32)
-    for i in range(halves):
-        for m in range(chips):
-            total = total + fin[i, m].astype(jnp.float32)
+            send(
+                fsend.at[dh, pm], frecv.at[halves - dh, pm],
+                fpart_ss.at[dh, j], fpart_rs.at[halves - dh, j], e, wrap(h, dh, halves),
+            )
+    arrived(prec.at[0], pair_rs.at[0])
+    for j, d in enumerate(order):
+        pm = wrap(chip, d, chips)
+        total = psend[0, parity, pm].astype(jnp.float32) + prec[0, pm].astype(jnp.float32)
+        for dh in others:
+            arrived(frecv.at[dh, pm], fpart_rs.at[dh, j])
+            total = total + frecv[dh, pm].astype(jnp.float32)
+        if d:
+            rsend[pm] = total.astype(jnp.bfloat16)
+            send(rsend.at[pm], fin.at[chip], fin_ss.at[j], fin_rs.at[chip], 2 * pm + parity, h)
+    for d in chips_near:
+        pm = wrap(chip, chips - d, chips)
+        arrived(fin.at[pm], fin_rs.at[pm])
+        total = total + fin[pm].astype(jnp.float32)
     gtok_ref[...] = total.astype(jnp.bfloat16)
     for c in sends:
         c.wait_send()
@@ -302,16 +358,22 @@
     tok, width = tokens.shape
     hidden = gate_weight.shape[2]
     rows, full, chips = n * tok, halves * width, n // 2
+    top = expert_ids.shape[1]
     low, wide = jnp.bfloat16, jnp.float32
     vmem, dma = pltpu.VMEM, pltpu.SemaphoreType.DMA
     local = pl.BlockSpec(memory_space=pltpu.VMEM)
     remain = pl.BlockSpec(memory_space=pl.ANY)
-    return pl.pallas_call(
+    result = [jax.ShapeDtypeStruct((tok, width), low)] * 2
+    outs = pl.pallas_call(
         functools.partial(fused_kernel, n, halves),
-        out_shape=[jax.ShapeDtypeStruct((tok, width), low)] * 2,
-        in_specs=[local] * 5 + [remain] * 3,
+        out_shape=result,
+        in_specs=[remain] * 8,
         out_specs=[local] * 2,
         scratch_shapes=[
+            vmem((tok, width), low),
+            vmem((top, tok), jnp.int32),
+            vmem((top, tok), wide),
+            vmem((1, tok), jnp.int32),
             vmem((halves, n, tok, width), low),
             vmem((full, hidden), low),
             vmem((full, hidden), low),
@@ -324,35 +386,47 @@
             vmem((halves, n, tok, width), low),
             vmem((halves, n, tok, width), low),
             vmem((n, tok, width), low),
+            vmem((n, tok, width), low),
+            vmem((n, tok, width), low),
             vmem((halves, n, rows), wide),
             vmem((n, tok, width), low),
             vmem((halves, n, tok, width), low),
-            vmem((2, halves, chips, tok, width), low),
+            vmem((halves, 2, chips, tok, width), low),
             vmem((halves, chips, tok, width), low),
             vmem((halves, chips, tok, width), low),
             vmem((halves, chips, tok, width), low),
-            dma((3,)),
-            dma((halves * n,)),
+            vmem((chips, tok, width), low),
+            vmem((chips, tok, width), low),
+            dma((8,)),
+            dma((2 * halves * n,)),
+            dma((halves, n)),
+            dma((halves, n)),
+            dma((halves, n)),
+            dma((n,)),
+            dma((n,)),
+            dma((halves,)),
+            dma((halves,)),
+            dma((n,)),
             dma((halves, n)),
             dma((halves * n,)),
-            dma((halves, n)),
             dma((halves,)),
             dma((halves,)),
-            dma((halves * n,)),
-            dma((halves, n)),
-            dma,
-            dma,
-            dma((halves * chips,)),
             dma((halves, chips)),
+            dma((halves, chips)),
+            dma((chips,)),
+            dma((chips,)),
         ],
         compiler_params=pltpu.CompilerParams(
             collective_id=0, has_side_effects=True, vmem_limit_bytes=56 * 1024 * 1024
         ),
         name="experts",
     )(
-        tokens, upstream, expert_ids, gate_probs, pad_mask.reshape(tok, 1),
+        tokens, upstream, expert_ids.T, gate_probs.T, pad_mask.reshape(1, tok),
         gate_weight, up_weight, down_weight,
     )
+    return pl.pallas_call(
+        copy_kernel, out_shape=result, in_specs=[local] * 2, out_specs=[local] * 2, name="results"
+    )(*outs)
 
 
 def shards(tokens, upstream, expert_ids, gate_probs, pad_mask, gate_weight, up_weight, down_weight):

time: 102 us -> 86.5 us (0.85); the launches traced: 100 us -> 86.3 us
  Pallas kernels: 92.9 us -> 85.7 us
  local copies, waits for them, and re-layouts: 6.79 us -> 0 us
    pallas_call x1 -> x2, Pallas kernels: 92.9 us -> 85.7 us  [the longest x1 84.3 us: fused(): pl.pallas_call(functools.partial(fused_kernel, n, halves), out_shape=resu...]
    unnamed x4 -> x0, local copies, waits for them, and re-layouts: 5.46 us -> none
    reshape x1 -> x0, local copies, waits for them, and re-layouts: 1.33 us -> none  [fused(): pad_mask.reshape(tok, 1)]
where the time goes in v2:
time: 86.5 us; the launch traced here: 86.3 us
  Pallas kernels  85.7 us (99%)
    pallas_call x1, Pallas kernels, fused(): pl.pallas_call(functools.partial(fused_kernel, n, halves), out_shape=resu...  84.3 us

profile of v2, /device:TPU:0, one launch (start us, length us, event | category | flops | bytes accessed | tf_op | source)
XLA Modules:
  0.0 86.3 jit_solution(4775641568383389346)
XLA Ops:
  0.6 84.3 %experts.1 = (bf16[16,1024]{1,0:T(8,128)(2,1)}, bf16[16,1024]{1,0:T(8,128)(2,1)}) custom-call(bf16[16,1024]{1,0:T(8,128)(2,1)} %tok_hbm.1, bf16[16,1024]{1,0:T(8,128)(2,1)} %up_hbm.1, s32[8,16]{1,0:T(8,128)} %bitcast.3, f32[8,16]{1,0:T(8,128)} %bitcast.4, s32[1,16]{1,0:T(1,128)} %bitcast.5, bf16[1,2048,768]{2,1,0:T(8,128)(2,1)} %wg_hbm.1, ...), custom_call_target="tpu_custom_call" | custom-call | tf_op jit(solution)/shard_map/experts/pallas_call | solution.py:367
  84.9 1.4 %results.1 = (bf16[16,1024]{1,0:T(8,128)(2,1)}, bf16[16,1024]{1,0:T(8,128)(2,1)}) custom-call(bf16[16,1024]{1,0:T(8,128)(2,1)} %get-tuple-element.4.a_ref, bf16[16,1024]{1,0:T(8,128)(2,1)} %get-tuple-element.5.b_ref), custom_call_target="tpu_custom_call" | custom-call | tf_op jit(solution)/shard_map/results/pallas_call | solution.py:427

commit v3 on v2

--- a/solution.py
+++ b/solution.py
@@ -71,7 +71,7 @@
     layer_ref, gtok_ref,
     up_ref, ids_ref, probs_ref, pad_ref,
     tok_buf, wg, wu, wd, gate_v, up_v, hid, gg, gu,
-    osend, orecv, ored, xrecv, xs, gram_s, gsend, grows, psend, prec, fsend, frecv, rsend, fin,
+    osend, orecv, ored, xrecv, xs, gram_s, whole_s, gsend, grows, psend, prec, fsend, frecv, rsend, fin,
     w_sem, tok_ss, tok_rs, part_ss, part_rs, out_ss, out_rs, gram_ss, gram_rs,
     grad_ss, grad_rs, relay_ss, pair_ss, pair_rs, fpart_ss, fpart_rs, fin_ss, fin_rs,
 ):
@@ -81,6 +81,7 @@
     hidden = wg.shape[1]
     rows = n * tok
     chips = n // 2
+    group = min(n, 8)
     parity = lax.rem(e, 2)
     chip = lax.div(e, 2)
     sibling = e + 1 - 2 * parity
@@ -95,6 +96,15 @@
     def wrap(a, d, size):
         return lax.rem(a + d, size)
 
+    def flip(a, d):
+        bit = 1
+        out = a
+        while bit <= d:
+            if d & bit:
+                out = out + bit * (1 - 2 * lax.rem(lax.div(a, bit), 2))
+            bit *= 2
+        return out
+
     def arrived(slot, rsem):
         remote(slot, slot, pair_ss.at[0], rsem, sibling, h).wait_recv()
 
@@ -115,15 +125,15 @@
         c.start()
 
     others = list(range(1, halves))
-    near = sorted(range(1, n), key=lambda d: (min(d, n - d), d))
+    near = list(range(1, n))
     outer = near[::-1]
-    chips_near = sorted(range(1, chips), key=lambda d: (min(d, chips - d), d))
+    chips_near = list(range(1, chips))
     chips_far = chips_near[::-1]
 
     barrier = pltpu.get_barrier_semaphore()
     for d in outer:
         pl.semaphore_signal(
-            barrier, inc=1, device_id=(wrap(e, d, n), h), device_id_type=pl.DeviceIdType.MESH
+            barrier, inc=1, device_id=(flip(e, d), h), device_id_type=pl.DeviceIdType.MESH
         )
     for d in others:
         pl.semaphore_signal(
@@ -135,7 +145,7 @@
     k = 0
     mine = tok_buf.at[h, e]
     for d in chips_far:
-        send(mine, mine, tok_ss.at[k], tok_rs.at[h, e], 2 * wrap(chip, d, chips) + parity, h)
+        send(mine, mine, tok_ss.at[k], tok_rs.at[h, e], 2 * flip(chip, d) + parity, h)
         k += 1
     for d in others:
         send(mine, mine, tok_ss.at[k], tok_rs.at[h, e], e, wrap(h, d, halves))
@@ -143,7 +153,7 @@
     send(mine, mine, tok_ss.at[k], tok_rs.at[h, e], sibling, h)
     k += 1
     for d in chips_near:
-        pe = 2 * wrap(chip, chips - d, chips) + parity
+        pe = 2 * flip(chip, d) + parity
         slot = tok_buf.at[h, pe]
         arrived(slot, tok_rs.at[h, pe])
         for dh in others:
@@ -152,7 +162,7 @@
         send(slot, slot, tok_ss.at[k], tok_rs.at[h, pe], sibling, h)
         k += 1
     for d in [0] + chips_near:
-        pe = 2 * wrap(chip, chips - d, chips) + parity
+        pe = 2 * flip(chip, d) + parity
         for dh in others:
             ph = wrap(h, halves - dh, halves)
             slot = tok_buf.at[ph, pe]
@@ -162,7 +172,7 @@
     for c in loads[1:7]:
         c.wait()
     for d in [0] + chips_near:
-        pe = 2 * wrap(chip, chips - d, chips) + 1 - parity
+        pe = 2 * flip(chip, d) + 1 - parity
         for ph in range(halves):
             arrived(tok_buf.at[ph, pe], tok_rs.at[ph, pe])
 
@@ -191,7 +201,7 @@
         tiles(width, down_step)
         if dh:
             for j, d in enumerate(outer + [0]):
-                pe = wrap(e, d, n)
+                pe = flip(e, d)
                 send(
                     osend.at[dh, pe], orecv.at[halves - dh, pe],
                     part_ss.at[dh, j], part_rs.at[halves - dh, j], e, ph,
@@ -214,13 +224,8 @@
         probs = jnp.where(lane == j, column(probs_ref[j:j + 1, :]), probs)
     pad = column(pad_ref[...].astype(jnp.float32))
     shares = probs / jnp.sum(probs, axis=1, keepdims=True)
-    named_rows, share_rows = [], []
-    for i in range(n):
-        named_rows.append(jnp.sum((ids == float(i)).astype(jnp.float32), axis=1, keepdims=True))
-        share_rows.append(jnp.sum(jnp.where(ids == float(i), shares, 0.0), axis=1, keepdims=True))
-
     for j, d in enumerate(outer + [0]):
-        pe = wrap(e, d, n)
+        pe = flip(e, d)
         total = osend[0, pe].astype(jnp.float32)
         for dh in others:
             arrived(orecv.at[dh, pe], part_rs.at[dh, j])
@@ -230,17 +235,19 @@
             send(ored.at[pe], xrecv.at[e], out_ss.at[j], out_rs.at[e], pe, h)
         else:
             xrecv[e] = total.astype(jnp.bfloat16)
-    for d in near:
-        pe = wrap(e, n - d, n)
-        arrived(xrecv.at[pe], out_rs.at[pe])
+    def share_of(i):
+        listed = (ids == i.astype(jnp.float32)).astype(jnp.float32)
+        return jnp.sum(listed * shares, axis=1, keepdims=True), jnp.sum(listed, axis=1, keepdims=True)
 
     layer = jnp.zeros((tok, width), jnp.float32)
-    for i in range(n):
-        value = xrecv[i]
-        value = jnp.where(named_rows[i] > 0.0, value.astype(jnp.float32), 0.0)
-        xs[i] = value.astype(jnp.bfloat16)
-        layer = layer + share_rows[i] * value
-    layer_ref[...] = layer.astype(jnp.bfloat16)
+    for d in [0] + near:
+        pe = flip(e, d)
+        share, listed = share_of(pe)
+        if d:
+            arrived(xrecv.at[pe], out_rs.at[pe])
+        value = jnp.where(listed > 0.0, xrecv[pe].astype(jnp.float32), 0.0)
+        xs[pe] = value.astype(jnp.bfloat16)
+        layer = layer + share * value
 
     x_all = xs[...].reshape(rows, width)
     same = (
@@ -262,36 +269,40 @@
         != lax.broadcasted_iota(jnp.int32, (n, rows), 0)
     ).astype(jnp.float32)
     whole = whole * (apart * (orth_weight / math.sqrt(full)))
-    coeffs = (whole[:, None, :] * same[None]).reshape(rows, rows)
-    high = coeffs.astype(jnp.bfloat16)
-    low = (coeffs - high.astype(jnp.float32)).astype(jnp.bfloat16)
-
-    def grad_step(cols, size):
-        x = xs[:, :, cols].reshape(rows, size)
-        mixed = (dot(high, x) + dot(low, x)).reshape(n, tok, size)
-        upstream = up_ref[:, cols].astype(jnp.float32)
-        for i in range(n):
-            gsend[i, :, cols] = (pad * (share_rows[i] * upstream + mixed[i])).astype(jnp.bfloat16)
-
-    tiles(width, grad_step)
-
-    for j, d in enumerate(outer):
-        pe = wrap(e, d, n)
-        send(gsend.at[pe], grows.at[h, e], grad_ss.at[j], grad_rs.at[h, e], pe, h)
-    k = 0
-    for dh in others:
-        send(gsend.at[e], grows.at[h, e], relay_ss.at[k], grad_rs.at[h, e], e, wrap(h, dh, halves))
-        k += 1
+    whole_s[...] = whole
+    x_all = xs[...].reshape(rows, width)
+    upstream = up_ref[...].astype(jnp.float32)
+    for g in range(n // group):
+        first = pl.multiple_of(flip(lax.div(e, group), g) * group, group)
+        coeffs = whole_s[pl.ds(first, group), :][:, None, :] * same[None]
+        coeffs = coeffs.reshape(group * tok, rows)
+        high = coeffs.astype(jnp.bfloat16)
+        low = (coeffs - high.astype(jnp.float32)).astype(jnp.bfloat16)
+        mixed = (dot(high, x_all) + dot(low, x_all)).reshape(group, tok, width)
+        for i in range(group):
+            share, _ = share_of(first + i)
+            gsend[first + i] = (pad * (share * upstream + mixed[i])).astype(jnp.bfloat16)
+        for d in range(max(1, g * group), (g + 1) * group):
+            pe = flip(e, d)
+            send(gsend.at[pe], grows.at[h, e], grad_ss.at[d], grad_rs.at[h, e], pe, h)
+        if g == 0:
+            for dh in others:
+                send(
+                    gsend.at[e], grows.at[h, e], relay_ss.at[dh - 1], grad_rs.at[h, e],
+                    e, wrap(h, dh, halves),
+                )
+    layer_ref[...] = layer.astype(jnp.bfloat16)
+    k = len(others)
     grows[h, e] = gsend[e]
     for d in near:
-        pe = wrap(e, n - d, n)
+        pe = flip(e, d)
         slot = grows.at[h, pe]
         arrived(slot, grad_rs.at[h, pe])
         for dh in others:
             send(slot, slot, relay_ss.at[k], grad_rs.at[h, pe], e, wrap(h, dh, halves))
             k += 1
     for d in [0] + near:
-        pe = wrap(e, n - d, n)
+        pe = flip(e, d)
         for dh in others:
             ph = wrap(h, halves - dh, halves)
             arrived(grows.at[ph, pe], grad_rs.at[ph, pe])
@@ -326,7 +337,7 @@
     for dh in others:
         arrived(prec.at[dh], pair_rs.at[dh])
         for j, d in enumerate(order):
-            pm = wrap(chip, d, chips)
+            pm = flip(chip, d)
             fsend[dh, pm] = (
                 psend[dh, parity, pm].astype(jnp.float32) + prec[dh, pm].astype(jnp.float32)
             ).astype(jnp.bfloat16)
@@ -336,7 +347,7 @@
             )
     arrived(prec.at[0], pair_rs.at[0])
     for j, d in enumerate(order):
-        pm = wrap(chip, d, chips)
+        pm = flip(chip, d)
         total = psend[0, parity, pm].astype(jnp.float32) + prec[0, pm].astype(jnp.float32)
         for dh in others:
             arrived(frecv.at[dh, pm], fpart_rs.at[dh, j])
@@ -345,7 +356,7 @@
             rsend[pm] = total.astype(jnp.bfloat16)
             send(rsend.at[pm], fin.at[chip], fin_ss.at[j], fin_rs.at[chip], 2 * pm + parity, h)
     for d in chips_near:
-        pm = wrap(chip, chips - d, chips)
+        pm = flip(chip, d)
         arrived(fin.at[pm], fin_rs.at[pm])
         total = total + fin[pm].astype(jnp.float32)
     gtok_ref[...] = total.astype(jnp.bfloat16)
@@ -389,6 +400,7 @@
             vmem((n, tok, width), low),
             vmem((n, tok, width), low),
             vmem((halves, n, rows), wide),
+            vmem((n, rows), wide),
             vmem((n, tok, width), low),
             vmem((halves, n, tok, width), low),
             vmem((halves, 2, chips, tok, width), low),
@@ -433,7 +445,7 @@
     tok_count, top_count = expert_ids.shape
     experts = lax.axis_size("expert")
     capacity = min(tok_count, 2 * tok_count * top_count // experts)
-    if capacity == tok_count and experts % 2 == 0:
+    if capacity == tok_count and experts > 1 and experts & (experts - 1) == 0:
         return fused(
             tokens, upstream, expert_ids, gate_probs, pad_mask, gate_weight, up_weight, down_weight
         )

time: 86.5 us -> 79 us (0.913)
  Pallas kernels: 85.7 us -> 78.2 us
    pallas_call x1, Pallas kernels: 84.3 us -> 76.8 us  [fused(): pl.pallas_call(functools.partial(fused_kernel, n, halves), out_shape=resu...]
where the time goes in v3:
time: 79 us; the launch traced here: 78.8 us
  Pallas kernels  78.2 us (99%)
    pallas_call x1, Pallas kernels, fused(): pl.pallas_call(functools.partial(fused_kernel, n, halves), out_shape=resu...  76.8 us

profile of v3, /device:TPU:0, one launch (start us, length us, event | category | flops | bytes accessed | tf_op | source)
XLA Modules:
  0.0 78.8 jit_solution(7279413006867472450)
XLA Ops:
  0.6 76.8 %experts.1 = (bf16[16,1024]{1,0:T(8,128)(2,1)}, bf16[16,1024]{1,0:T(8,128)(2,1)}) custom-call(bf16[16,1024]{1,0:T(8,128)(2,1)} %tok_hbm.1, bf16[16,1024]{1,0:T(8,128)(2,1)} %up_hbm.1, s32[8,16]{1,0:T(8,128)} %bitcast.3, f32[8,16]{1,0:T(8,128)} %bitcast.4, s32[1,16]{1,0:T(1,128)} %bitcast.5, bf16[1,2048,768]{2,1,0:T(8,128)(2,1)} %wg_hbm.1, ...), custom_call_target="tpu_custom_call" | custom-call | tf_op jit(solution)/shard_map/experts/pallas_call | solution.py:378
  77.4 1.4 %results.1 = (bf16[16,1024]{1,0:T(8,128)(2,1)}, bf16[16,1024]{1,0:T(8,128)(2,1)}) custom-call(bf16[16,1024]{1,0:T(8,128)(2,1)} %get-tuple-element.4.a_ref, bf16[16,1024]{1,0:T(8,128)(2,1)} %get-tuple-element.5.b_ref), custom_call_target="tpu_custom_call" | custom-call | tf_op jit(solution)/shard_map/results/pallas_call | solution.py:439

commit v4 on v3

--- a/solution.py
+++ b/solution.py
@@ -70,7 +70,7 @@
     tok_hbm, up_hbm, ids_hbm, probs_hbm, pad_hbm, wg_hbm, wu_hbm, wd_hbm,
     layer_ref, gtok_ref,
     up_ref, ids_ref, probs_ref, pad_ref,
-    tok_buf, wg, wu, wd, gate_v, up_v, hid, gg, gu,
+    tok_buf, wg, wu, wd, gate_v, up_v, act_v, hid, gg, gu,
     osend, orecv, ored, xrecv, xs, gram_s, whole_s, gsend, grows, psend, prec, fsend, frecv, rsend, fin,
     w_sem, tok_ss, tok_rs, part_ss, part_rs, out_ss, out_rs, gram_ss, gram_rs,
     grad_ss, grad_rs, relay_ss, pair_ss, pair_rs, fpart_ss, fpart_rs, fin_ss, fin_rs,
@@ -144,7 +144,7 @@
     loads[0].wait()
     k = 0
     mine = tok_buf.at[h, e]
-    for d in chips_far:
+    for d in [d for d in chips_far if d % 2 == 0 or d == 1]:
         send(mine, mine, tok_ss.at[k], tok_rs.at[h, e], 2 * flip(chip, d) + parity, h)
         k += 1
     for d in others:
@@ -152,16 +152,21 @@
         k += 1
     send(mine, mine, tok_ss.at[k], tok_rs.at[h, e], sibling, h)
     k += 1
-    for d in chips_near:
+    coming = sorted(chips_near, key=lambda d: (d // 4, d % 2, d))
+    for d in coming:
         pe = 2 * flip(chip, d) + parity
         slot = tok_buf.at[h, pe]
         arrived(slot, tok_rs.at[h, pe])
+        if d % 2 == 0:
+            beside = 2 * flip(chip, 1) + parity
+            send(slot, slot, tok_ss.at[k], tok_rs.at[h, pe], beside, h)
+            k += 1
         for dh in others:
             send(slot, slot, tok_ss.at[k], tok_rs.at[h, pe], e, wrap(h, dh, halves))
             k += 1
         send(slot, slot, tok_ss.at[k], tok_rs.at[h, pe], sibling, h)
         k += 1
-    for d in [0] + chips_near:
+    for d in [0] + coming:
         pe = 2 * flip(chip, d) + parity
         for dh in others:
             ph = wrap(h, halves - dh, halves)
@@ -171,23 +176,26 @@
             k += 1
     for c in loads[1:7]:
         c.wait()
-    for d in [0] + chips_near:
-        pe = 2 * flip(chip, d) + 1 - parity
-        for ph in range(halves):
+    for dh in [0] + others:
+        ph = wrap(h, halves - dh, halves)
+        for d in [0] + coming:
+            pe = 2 * flip(chip, d) + 1 - parity
             arrived(tok_buf.at[ph, pe], tok_rs.at[ph, pe])
 
-    def hidden_step(cols, size):
-        gate = jnp.zeros((rows, size), jnp.float32)
-        up = jnp.zeros((rows, size), jnp.float32)
-        for i in range(halves):
-            x = tok_buf[i].reshape(rows, width)
-            gate = gate + dot(x, wg[i * width:(i + 1) * width, cols])
-            up = up + dot(x, wu[i * width:(i + 1) * width, cols])
-        gate_v[:, cols] = gate
-        up_v[:, cols] = up
-        hid[:, cols] = (gate / (1.0 + jnp.exp(-gate)) * up).astype(jnp.bfloat16)
-
-    tiles(hidden, hidden_step)
+        def hidden_step(cols, size, ph=ph, dh=dh):
+            at = pl.ds(pl.multiple_of(ph * width, width), width)
+            x = tok_buf[ph].reshape(rows, width)
+            gate = dot(x, wg[at, cols])
+            up = dot(x, wu[at, cols])
+            if dh:
+                gate = gate + gate_v[:, cols]
+                up = up + up_v[:, cols]
+            gate_v[:, cols] = gate
+            up_v[:, cols] = up
+            if dh == halves - 1:
+                hid[:, cols] = (gate / (1.0 + jnp.exp(-gate)) * up).astype(jnp.bfloat16)
+
+        tiles(hidden, hidden_step)
     loads[7].wait()
 
     for dh in others + [0]:
@@ -301,25 +309,29 @@
         for dh in others:
             send(slot, slot, relay_ss.at[k], grad_rs.at[h, pe], e, wrap(h, dh, halves))
             k += 1
-    for d in [0] + near:
-        pe = flip(e, d)
-        for dh in others:
-            ph = wrap(h, halves - dh, halves)
-            arrived(grows.at[ph, pe], grad_rs.at[ph, pe])
-
-    def act_step(cols, size):
-        act = jnp.zeros((rows, size), jnp.float32)
-        for i in range(halves):
-            g = grows[i].reshape(rows, width)
-            act = act + dot_t(g, wd[cols, i * width:(i + 1) * width])
-        gate = gate_v[:, cols]
-        sigma = 1.0 / (1.0 + jnp.exp(-gate))
-        gg[:, cols] = (
-            act * up_v[:, cols] * sigma * (1.0 + gate * (1.0 - sigma))
-        ).astype(jnp.bfloat16)
-        gu[:, cols] = (act * gate * sigma).astype(jnp.bfloat16)
-
-    tiles(hidden, act_step)
+    for dh in [0] + others:
+        ph = wrap(h, halves - dh, halves)
+        if dh:
+            for d in [0] + near:
+                pe = flip(e, d)
+                arrived(grows.at[ph, pe], grad_rs.at[ph, pe])
+
+        def act_step(cols, size, ph=ph, dh=dh):
+            at = pl.ds(pl.multiple_of(ph * width, width), width)
+            act = dot_t(grows[ph].reshape(rows, width), wd[cols, at])
+            if dh:
+                act = act + act_v[:, cols]
+            if dh < halves - 1:
+                act_v[:, cols] = act
+            else:
+                gate = gate_v[:, cols]
+                sigma = 1.0 / (1.0 + jnp.exp(-gate))
+                gg[:, cols] = (
+                    act * up_v[:, cols] * sigma * (1.0 + gate * (1.0 - sigma))
+                ).astype(jnp.bfloat16)
+                gu[:, cols] = (act * gate * sigma).astype(jnp.bfloat16)
+
+        tiles(hidden, act_step)
 
     for dh in others + [0]:
         ph = wrap(h, dh, halves)
@@ -389,6 +401,7 @@
             vmem((full, hidden), low),
             vmem((full, hidden), low),
             vmem((hidden, full), low),
+            vmem((rows, hidden), wide),
             vmem((rows, hidden), wide),
             vmem((rows, hidden), wide),
             vmem((rows, hidden), low),

time: 79 us -> 80 us (1.013)
  Pallas kernels: 78.2 us -> 79.2 us
    pallas_call x1, Pallas kernels: 76.8 us -> 77.8 us  [fused(): pl.pallas_call(functools.partial(fused_kernel, n, halves), out_shape=resu...]
where the time goes in v4:
time: 80 us; the launch traced here: 79.8 us
  Pallas kernels  79.2 us (99%)
    pallas_call x1, Pallas kernels, fused(): pl.pallas_call(functools.partial(fused_kernel, n, halves), out_shape=resu...  77.8 us

profile of v4, /device:TPU:0, one launch (start us, length us, event | category | flops | bytes accessed | tf_op | source)
XLA Modules:
  0.0 79.8 jit_solution(9236203699489628678)
XLA Ops:
  0.6 77.8 %experts.1 = (bf16[16,1024]{1,0:T(8,128)(2,1)}, bf16[16,1024]{1,0:T(8,128)(2,1)}) custom-call(bf16[16,1024]{1,0:T(8,128)(2,1)} %tok_hbm.1, bf16[16,1024]{1,0:T(8,128)(2,1)} %up_hbm.1, s32[8,16]{1,0:T(8,128)} %bitcast.3, f32[8,16]{1,0:T(8,128)} %bitcast.4, s32[1,16]{1,0:T(1,128)} %bitcast.5, bf16[1,2048,768]{2,1,0:T(8,128)(2,1)} %wg_hbm.1, ...), custom_call_target="tpu_custom_call" | custom-call | tf_op jit(solution)/shard_map/experts/pallas_call | solution.py:390
  78.4 1.4 %results.1 = (bf16[16,1024]{1,0:T(8,128)(2,1)}, bf16[16,1024]{1,0:T(8,128)(2,1)}) custom-call(bf16[16,1024]{1,0:T(8,128)(2,1)} %get-tuple-element.4.a_ref, bf16[16,1024]{1,0:T(8,128)(2,1)} %get-tuple-element.5.b_ref), custom_call_target="tpu_custom_call" | custom-call | tf_op jit(solution)/shard_map/results/pallas_call | solution.py:452

commit v5 on v4

--- a/solution.py
+++ b/solution.py
@@ -144,7 +144,7 @@
     loads[0].wait()
     k = 0
     mine = tok_buf.at[h, e]
-    for d in [d for d in chips_far if d % 2 == 0 or d == 1]:
+    for d in chips_far:
         send(mine, mine, tok_ss.at[k], tok_rs.at[h, e], 2 * flip(chip, d) + parity, h)
         k += 1
     for d in others:
@@ -152,21 +152,16 @@
         k += 1
     send(mine, mine, tok_ss.at[k], tok_rs.at[h, e], sibling, h)
     k += 1
-    coming = sorted(chips_near, key=lambda d: (d // 4, d % 2, d))
-    for d in coming:
+    for d in chips_near:
         pe = 2 * flip(chip, d) + parity
         slot = tok_buf.at[h, pe]
         arrived(slot, tok_rs.at[h, pe])
-        if d % 2 == 0:
-            beside = 2 * flip(chip, 1) + parity
-            send(slot, slot, tok_ss.at[k], tok_rs.at[h, pe], beside, h)
-            k += 1
         for dh in others:
             send(slot, slot, tok_ss.at[k], tok_rs.at[h, pe], e, wrap(h, dh, halves))
             k += 1
         send(slot, slot, tok_ss.at[k], tok_rs.at[h, pe], sibling, h)
         k += 1
-    for d in [0] + coming:
+    for d in [0] + chips_near:
         pe = 2 * flip(chip, d) + parity
         for dh in others:
             ph = wrap(h, halves - dh, halves)
@@ -178,7 +173,7 @@
         c.wait()
     for dh in [0] + others:
         ph = wrap(h, halves - dh, halves)
-        for d in [0] + coming:
+        for d in [0] + chips_near:
             pe = 2 * flip(chip, d) + 1 - parity
             arrived(tok_buf.at[ph, pe], tok_rs.at[ph, pe])
 

time: 80 us -> 78.5 us (0.981)
  Pallas kernels: 79.2 us -> 77.6 us
    pallas_call x1, Pallas kernels: 77.8 us -> 76.2 us  [fused(): pl.pallas_call(functools.partial(fused_kernel, n, halves), out_shape=resu...]
where the time goes in v5:
time: 78.5 us; the launch traced here: 78.3 us
  Pallas kernels  77.6 us (99%)
    pallas_call x1, Pallas kernels, fused(): pl.pallas_call(functools.partial(fused_kernel, n, halves), out_shape=resu...  76.2 us

profile of v5, /device:TPU:0, one launch (start us, length us, event | category | flops | bytes accessed | tf_op | source)
XLA Modules:
  0.0 78.3 jit_solution(13308271119655710484)
XLA Ops:
  0.6 76.2 %experts.1 = (bf16[16,1024]{1,0:T(8,128)(2,1)}, bf16[16,1024]{1,0:T(8,128)(2,1)}) custom-call(bf16[16,1024]{1,0:T(8,128)(2,1)} %tok_hbm.1, bf16[16,1024]{1,0:T(8,128)(2,1)} %up_hbm.1, s32[8,16]{1,0:T(8,128)} %bitcast.3, f32[8,16]{1,0:T(8,128)} %bitcast.4, s32[1,16]{1,0:T(1,128)} %bitcast.5, bf16[1,2048,768]{2,1,0:T(8,128)(2,1)} %wg_hbm.1, ...), custom_call_target="tpu_custom_call" | custom-call | tf_op jit(solution)/shard_map/experts/pallas_call | solution.py:385
  76.9 1.4 %results.1 = (bf16[16,1024]{1,0:T(8,128)(2,1)}, bf16[16,1024]{1,0:T(8,128)(2,1)}) custom-call(bf16[16,1024]{1,0:T(8,128)(2,1)} %get-tuple-element.4.a_ref, bf16[16,1024]{1,0:T(8,128)(2,1)} %get-tuple-element.5.b_ref), custom_call_target="tpu_custom_call" | custom-call | tf_op jit(solution)/shard_map/results/pallas_call | solution.py:447
